TPU v7x, 512 devices: a whole 4x4x16 slice. The times are simulated.
512 devices in a mesh: section: 4 (over z_hi), dp: 8 (over x, core), tensor: 16 (over z_lo, y).
Axes of the slice: x: 4, y: 4, z: 16 (z_hi: 4, z_lo: 4; z = z_hi * 4 + z_lo), core: 2. Of those that a mesh axis runs over, the one named last changes fastest.
Arguments:
- hidden: bfloat16 [4, 1024, 28672], P('section', 'tensor', 'dp'), may hold values from -6 to 6
- down_weight: bfloat16 [4, 28672, 8192], P('section', 'dp', 'tensor'), may hold values from -0.03125 to 0.03125
- residual: bfloat16 [4, 1024, 8192], P('section', 'dp', 'tensor'), may hold values from -36 to 36
- norm_gain: float32 [4, 8192], P('section', 'tensor'), may hold values from 0.4 to 1.2
- query_weight: bfloat16 [4, 8192, 4096], P('section', 'tensor', 'dp'), may hold values from -0.0625 to 0.0625
- key_value_weight: bfloat16 [4, 8192, 2048], P('section', 'tensor', 'dp'), may hold values from -0.0625 to 0.0625
Outputs:
- attention: bfloat16 [4, 1024, 4096], P('section', 'tensor', 'dp')
All inputs are finite; a program needn't handle non-finite values.
Results may differ from a plain program's by a relative error of at most 0.04.
Values may be sent and summed in bfloat16 or wider, within the bound.
A program may use at most 64 MiB of HBM per device.

v0:
```python
import jax
import jax.numpy as jnp
from jax import lax
from jax.sharding import PartitionSpec as P

D = 8192
HD = 128
ROPE_BASE = 500000.0
EPSILON = 1e-05


def passed_along(value, axis, steps):
    count = lax.axis_size(axis)
    pairs = [(source, (source + steps) % count) for source in range(count)]
    return lax.ppermute(value, axis, pairs)


def rotate(values, positions):
    half_dim = values.shape[-1] // 2
    frequency = ROPE_BASE ** (-jnp.arange(half_dim, dtype=jnp.float32) * 2.0 / values.shape[-1])
    angles = positions.astype(jnp.float32)[:, None] * frequency[None, :]
    cosine = jnp.cos(angles)[:, None, :]
    sine_part = jnp.sin(angles)[:, None, :]
    front_part = values[..., :half_dim]
    back_part = values[..., half_dim:]
    return jnp.concatenate(
        [front_part * cosine - back_part * sine_part, back_part * cosine + front_part * sine_part],
        axis=-1,
    )


def per_device(hidden, down_weight, residual, norm_gain, query_weight, key_value_weight):
    weight_block = down_weight[0]
    partials = jnp.dot(
        lax.all_gather(hidden[0], "tensor", axis=0, tiled=True),
        weight_block,
        preferred_element_type=jnp.float32,
    )
    summed = lax.psum_scatter(
        partials.astype(jnp.bfloat16), "dp", scatter_dimension=0, tiled=True
    ).astype(jnp.float32)
    boundary = (residual[0].astype(jnp.float32) + summed).astype(jnp.bfloat16)
    gathered = lax.all_gather(boundary, "dp", axis=0, tiled=True)
    arrived = passed_along(gathered, "section", 1)
    values_in = arrived.astype(jnp.float32)
    squares = jnp.sum(values_in * values_in, axis=1)
    scaled = (values_in * norm_gain[0][None, :]).astype(jnp.bfloat16)
    query_sums = jnp.dot(scaled, query_weight[0], preferred_element_type=jnp.float32)
    pair_sums = jnp.dot(scaled, key_value_weight[0], preferred_element_type=jnp.float32)
    token_count = arrived.shape[0]
    own_rows = token_count // lax.axis_size("tensor")
    first_row = lax.axis_index("tensor") * own_rows
    query_sums, pair_sums, squares = (
        lax.psum(query_sums.astype(jnp.bfloat16), "tensor").astype(jnp.float32),
        lax.psum(pair_sums.astype(jnp.bfloat16), "tensor").astype(jnp.float32),
        lax.psum(squares.astype(jnp.bfloat16), "tensor").astype(jnp.float32),
    )
    query_local = lax.dynamic_slice_in_dim(query_sums, first_row, own_rows, 0)
    inverse = lax.rsqrt(squares / D + EPSILON)[:, None]
    positions = jnp.arange(token_count, dtype=jnp.int32)
    own_positions = first_row + jnp.arange(own_rows, dtype=jnp.int32)
    inverse_own = lax.dynamic_slice_in_dim(inverse, first_row, own_rows, 0)
    query_part = query_local * inverse_own
    queries = rotate(query_part.reshape(own_rows, -1, HD), own_positions).astype(jnp.bfloat16)
    pair_rows = (pair_sums * inverse).reshape(token_count, -1, 2, HD)
    key_rows = rotate(pair_rows[:, :, 0], positions).astype(jnp.bfloat16)
    value_rows = pair_rows[:, :, 1].astype(jnp.bfloat16)
    group_count = key_rows.shape[1]
    grouped = queries.reshape(own_rows, group_count, -1, HD)
    scores = jnp.einsum(
        "qgrd,kgd->grqk", grouped, key_rows, preferred_element_type=jnp.float32
    ) * HD ** (-0.5)
    causal = positions[None, :] <= own_positions[:, None]
    scores = jnp.where(causal[None, None], scores, -1e30)
    maximum = jnp.max(scores, axis=-1, keepdims=True)
    weights = jnp.exp(scores - maximum)
    probabilities = (weights / jnp.sum(weights, axis=-1, keepdims=True)).astype(jnp.bfloat16)
    attended = jnp.einsum(
        "grqk,kgd->qgrd", probabilities, value_rows, preferred_element_type=jnp.float32
    ).astype(jnp.bfloat16)
    return attended.reshape(own_rows, -1)[None]


def solution(mesh):
    placed = (
        P("section", "tensor", "dp"),
        P("section", "dp", "tensor"),
        P("section", "dp", "tensor"),
        P("section", "tensor"),
        P("section", "tensor", "dp"),
        P("section", "tensor", "dp"),
    )
    return jax.shard_map(
        per_device,
        mesh=mesh,
        in_specs=placed,
        out_specs=P("section", "tensor", "dp"),
        check_vma=False,
    )
```

profile of v0, /device:TPU:2, one launch (start us, length us, event | category | flops | bytes accessed | tf_op | source)
XLA Modules:
  0.0 486.2 jit_solution(7943351588400073942)
XLA Ops:
  6.5 0.7 all-gather.6.cloned.1.call-update
  7.3 0.0 reduce-scatter.2.cloned.1.call-start
  7.3 108.6 %all-gather.6.cloned.1.call-done = bf16[1,1024,3584]{2,1,0:T(8,128)(2,1)} async-done(((bf16[1,64,3584]{2,1,0:T(8,128)(2,1)}), bf16[1,1024,3584]{2,1,0:T(8,128)(2,1)}) %all-gather.6.cloned.1.call-update) | async-done | bytes 7340048 | tf_op jit(solution)/shard_map/all_gather | solution.py:35
  115.9 9.1 %fusion.5 = bf16[1024,512]{1,0:T(8,128)(2,1)} fusion(bf16[1,3584,512]{2,1,0:T(8,128)(2,1)} %param.7, bf16[1,1024,3584]{2,1,0:T(8,128)(2,1)} %all-gather.6.cloned.1.call-done), kind=kOutput, calls=%fused_computation.7 | convolution fusion | flops 3758620672 | bytes 12058624 | tf_op jit(solution)/shard_map/dot_general | solution.py:34
  125.0 0.0 reduce-scatter.2.cloned.1.call-update
  125.0 0.0 all-gather.4.cloned.1.call-start
  125.0 33.0 %reduce-scatter.2.cloned.1.call-done = bf16[128,512]{1,0:T(8,128)(2,1)} async-done(((bf16[1024,512]{1,0:T(8,128)(2,1)}), bf16[128,512]{1,0:T(8,128)(2,1)}) %reduce-scatter.2.cloned.1.call-update) | async-done | bytes 131088 | tf_op jit(solution)/shard_map/reduce_scatter | solution.py:39
  158.0 1.6 fusion.30
  159.6 0.0 all-reduce.3.cloned.1.call-start
  159.7 32.3 %all-gather.4.cloned.1.call-done = bf16[1024,512]{1,0:T(8,128)(2,1)} async-done(((bf16[128,512]{1,0:T(8,128)(2,1)}), bf16[1024,512]{1,0:T(8,128)(2,1)}) %all-gather.4.cloned.1.call-update) | async-done | bytes 1048592 | tf_op jit(solution)/shard_map/all_gather | solution.py:43
  192.0 7.2 %collective-permute-start = (bf16[1024,512]{1,0:T(8,128)(2,1)}, bf16[1024,512]{1,0:T(8,128)(2,1)S(1)}, u32[]{:S(2)}, u32[]{:S(2)}) collective-permute-start(bf16[1024,512]{1,0:T(8,128)(2,1)} %all-gather.4.cloned.1.call-done), channel_id=1, source_target_pairs={{0,128},{128,256},{256,384},{384,0},{1,129},{129,257},{257,385},{3... | collective-permute-start | bytes 3145736 | tf_op jit(solution)/shard_map/ppermute | solution.py:15
  199.2 55.4 %collective-permute-done = bf16[1024,512]{1,0:T(8,128)(2,1)S(1)} collective-permute-done((bf16[1024,512]{1,0:T(8,128)(2,1)}, bf16[1024,512]{1,0:T(8,128)(2,1)S(1)}, u32[]{:S(2)}, u32[]{:S(2)}) %collective-permute-start) | collective-permute-done | bytes 1048608 | tf_op jit(solution)/shard_map/ppermute | solution.py:15
  254.6 1.3 convolution_convert_fusion.1
  255.8 1.8 convolution_convert_fusion
  257.7 0.1 iota_compare_fusion
  257.8 0.2 multiply_cosine_fusion.1
  258.0 0.3 fusion.4
  258.2 79.6 %psum.22 = bf16[1024]{0:T(1024)(128)(2,1)S(1)} all-reduce(bf16[1024]{0:T(1024)(128)(2,1)S(1)} %fusion.4), channel_id=1, replica_groups=mesh['section'=4,'dp'=8,'tensor'=16] {'tensor'}, use_global_device_ids=true, to_apply=%region_3.0 | all-reduce | flops 1024 | bytes 4096 | tf_op jit(solution)/shard_map/psum | solution.py:56
  337.8 0.1 dynamic-slice.3
  337.9 133.5 %all-reduce.3.cloned.1.call-done = (bf16[1024,256]{1,0:T(8,128)(2,1)}, bf16[1024,512]{1,0:T(8,128)(2,1)}) async-done(((bf16[1024,256]{1,0:T(8,128)(2,1)}, bf16[1024,512]{1,0:T(8,128)(2,1)}), (bf16[1024,256]{1,0:T(8,128)(2,1)}, bf16[1024,512]{1,0:T(8,128)(2,1)})) %all-reduce.3.cloned.1.call-update) | async-done | bytes 1572880 | tf_op jit(solution)/shard_map/psum | solution.py:55
  471.5 1.2 convert_multiply_fusion.2
  472.7 0.5 reshape.223
  473.3 0.4 slice.26
  473.6 0.5 slice.25
  474.2 0.9 convert_multiply_fusion.3
  475.2 0.1 fusion.39
  475.3 2.4 fusion.33
  477.8 0.5 fusion.40
  478.3 0.3 fusion.13
  478.6 0.4 fusion.12
  479.0 0.1 copy.15
  479.1 0.7 broadcast_in_dim_reshape.3
  (18 shorter events, 0.2 us)
Async XLA Ops:
  6.5 249.3 %copy-start = (bf16[1,512,512]{2,1,0:T(8,128)(2,1)S(1)}, bf16[1,512,512]{2,1,0:T(8,128)(2,1)}, u32[]{:S(2)}) copy-start(bf16[1,512,512]{2,1,0:T(8,128)(2,1)} %param.10) | copy-start | bytes 1572868
  6.5 109.4 %all-gather.6.cloned.1.call-start = ((), (), s32[]{:S(2)}) async-start(), calls=%async_computation.3 | async-start | bytes 7798784 | tf_op jit(solution)/shard_map/all_gather | solution.py:35
  7.3 150.7 %copy-start.1 = (bf16[1,128,512]{2,1,0:T(8,128)(2,1)S(1)}, bf16[1,128,512]{2,1,0:T(8,128)(2,1)}, u32[]{:S(2)}) copy-start(bf16[1,128,512]{2,1,0:T(8,128)(2,1)} %param.8) | copy-start | bytes 393220
  7.3 247.3 %copy-start.2 = (bf16[1,512,256]{2,1,0:T(8,128)(2,1)S(1)}, bf16[1,512,256]{2,1,0:T(8,128)(2,1)}, u32[]{:S(2)}) copy-start(bf16[1,512,256]{2,1,0:T(8,128)(2,1)} %param.11) | copy-start | bytes 786436
  7.3 247.3 %copy-start.3 = (f32[1,512]{1,0:T(1,128)S(1)}, f32[1,512]{1,0:T(1,128)}, u32[]{:S(2)}) copy-start(f32[1,512]{1,0:T(1,128)} %param.9) | copy-start | bytes 6148
  7.3 150.7 %reduce-scatter.2.cloned.1.call-start = ((), (), s32[]{:S(2)}) async-start(), calls=%async_computation.1 | async-start | bytes 1179648 | tf_op jit(solution)/shard_map/reduce_scatter | solution.py:39
  125.0 67.0 %all-gather.4.cloned.1.call-start = ((), (), s32[]{:S(2)}) async-start(), calls=%async_computation.2 | async-start | bytes 1179648 | tf_op jit(solution)/shard_map/all_gather | solution.py:43
  159.6 311.9 %all-reduce.3.cloned.1.call-start = ((), (), s32[]{:S(2)}) async-start(), calls=%async_computation.4 | async-start | bytes 3145728 | tf_op jit(solution)/shard_map/psum | solution.py:55
  192.0 62.6 %collective-permute-start = (bf16[1024,512]{1,0:T(8,128)(2,1)}, bf16[1024,512]{1,0:T(8,128)(2,1)S(1)}, u32[]{:S(2)}, u32[]{:S(2)}) collective-permute-start(bf16[1024,512]{1,0:T(8,128)(2,1)} %all-gather.4.cloned.1.call-done), channel_id=1, source_target_pairs={{0,128},{128,256},{256,384},{384,0},{1,129},{129,257},{257,385},{3... | collective-permute-start | bytes 3145736 | tf_op jit(solution)/shard_map/ppermute | solution.py:15
Sparse Core Ops, SparseCore 0:
  9.4 106.4 all-gather.5
  125.1 32.8 reduce-scatter.1
  160.1 31.7 all-gather.3
  257.7 213.6 all-reduce.2
where the time goes:
time: 486 us
  waiting for transfers between devices  364 us (75%)
  blocking collectives  79.6 us (16%)
  between operations  13.3 us (3%)
  matrix products  12.9 us (3%)
  starting transfers between devices  7.32 us (2%)
  other arithmetic  7.13 us (1%)
    psum x1, waiting for transfers between devices, per_device(): lax.psum(pair_sums.astype(jnp.bfloat16), 'tensor').astype(jnp.float32)  134 us
    all_gather x1, waiting for transfers between devices, per_device(): lax.all_gather(hidden[0], 'tensor', axis=0, tiled=True)  109 us
    psum x1, blocking collectives, per_device(): lax.psum(squares.astype(jnp.bfloat16), 'tensor').astype(jnp.float32)  79.6 us
    ppermute x1, waiting for transfers between devices, passed_along(): return lax.ppermute(value, axis, pairs)  55.4 us
    reduce_scatter x1, waiting for transfers between devices, per_device(): lax.psum_scatter(partials.astype(jnp.bfloat16), 'dp', scatter_dimension=0...  33 us
    all_gather x1, waiting for transfers between devices, per_device(): gathered = lax.all_gather(boundary, 'dp', axis=0, tiled=True)  32.3 us
  transfers between devices with their start and end apart: 5, of which 5 were waited for; matrix products, arithmetic and copies ran while one was open for 0% of the time, Pallas kernels for 0%

commit v1 on v0

--- a/solution.py
+++ b/solution.py
@@ -52,7 +52,9 @@
     first_row = lax.axis_index("tensor") * own_rows
     query_sums, pair_sums, squares = (
         lax.psum(query_sums.astype(jnp.bfloat16), "tensor").astype(jnp.float32),
-        lax.psum(pair_sums.astype(jnp.bfloat16), "tensor").astype(jnp.float32),
+        jnp.sum(lax.all_gather(pair_sums.astype(jnp.bfloat16), "tensor"), axis=0).astype(
+            jnp.float32
+        ),
         lax.psum(squares.astype(jnp.bfloat16), "tensor").astype(jnp.float32),
     )
     query_local = lax.dynamic_slice_in_dim(query_sums, first_row, own_rows, 0)

time: 486 us -> 594 us (1.22)
  the two profiles are of different devices: /device:TPU:2 before, /device:TPU:1 now
where the time goes in v1:
time: 594 us; the launch traced here: 593 us
  waiting for transfers between devices  474 us (80%)
  blocking collectives  73.4 us (12%)
  between operations  13.3 us (2%)
  matrix products  12.9 us (2%)
  other arithmetic  10.9 us (2%)
  starting transfers between devices  7.35 us (1%)
    psum x1, waiting for transfers between devices, per_device(): lax.psum(query_sums.astype(jnp.bfloat16), 'tensor').astype(jnp.float32)  124 us
    all_gather x1, waiting for transfers between devices, per_device(): lax.all_gather(pair_sums.astype(jnp.bfloat16), 'tensor')  117 us
    all_gather x1, waiting for transfers between devices, per_device(): lax.all_gather(hidden[0], 'tensor', axis=0, tiled=True)  103 us
    psum x1, blocking collectives, per_device(): lax.psum(squares.astype(jnp.bfloat16), 'tensor').astype(jnp.float32)  73.4 us
    ppermute x1, waiting for transfers between devices, passed_along(): return lax.ppermute(value, axis, pairs)  55.1 us
    reduce_scatter x1, waiting for transfers between devices, per_device(): lax.psum_scatter(partials.astype(jnp.bfloat16), 'dp', scatter_dimension=0...  40.9 us
    all_gather x1, waiting for transfers between devices, per_device(): gathered = lax.all_gather(boundary, 'dp', axis=0, tiled=True)  32.7 us
  transfers between devices with their start and end apart: 6, of which 6 were waited for; matrix products, arithmetic and copies ran while one was open for 1% of the time, Pallas kernels for 0%

profile of v1, /device:TPU:1, one launch (start us, length us, event | category | flops | bytes accessed | tf_op | source)
XLA Modules:
  0.0 593.3 jit_solution(13348854013623134467)
XLA Ops:
  6.5 0.7 all-gather.8.cloned.1.call-update
  7.3 102.9 %all-gather.8.cloned.1.call-done = bf16[1,1024,3584]{2,1,0:T(8,128)(2,1)} async-done(((bf16[1,64,3584]{2,1,0:T(8,128)(2,1)}), bf16[1,1024,3584]{2,1,0:T(8,128)(2,1)}) %all-gather.8.cloned.1.call-update) | async-done | bytes 7340048 | tf_op jit(solution)/shard_map/all_gather | solution.py:35
  110.2 9.1 %fusion.5 = bf16[1024,512]{1,0:T(8,128)(2,1)} fusion(bf16[1,3584,512]{2,1,0:T(8,128)(2,1)} %param.7, bf16[1,1024,3584]{2,1,0:T(8,128)(2,1)} %all-gather.8.cloned.1.call-done), kind=kOutput, calls=%fused_computation.7 | convolution fusion | flops 3758620672 | bytes 12058624 | tf_op jit(solution)/shard_map/dot_general | solution.py:34
  119.3 0.0 all-gather.6.cloned.1.call-start
  119.3 40.9 %reduce-scatter.2.cloned.1.call-done = bf16[128,512]{1,0:T(8,128)(2,1)} async-done(((bf16[1024,512]{1,0:T(8,128)(2,1)}), bf16[128,512]{1,0:T(8,128)(2,1)}) %reduce-scatter.2.cloned.1.call-update) | async-done | bytes 131088 | tf_op jit(solution)/shard_map/reduce_scatter | solution.py:39
  160.3 1.6 fusion.30
  161.9 0.0 all-reduce.2.cloned.1.call-start
  161.9 32.7 %all-gather.6.cloned.1.call-done = bf16[1024,512]{1,0:T(8,128)(2,1)} async-done(((bf16[128,512]{1,0:T(8,128)(2,1)}), bf16[1024,512]{1,0:T(8,128)(2,1)}) %all-gather.6.cloned.1.call-update) | async-done | bytes 1048592 | tf_op jit(solution)/shard_map/all_gather | solution.py:43
  194.6 7.2 %collective-permute-start = (bf16[1024,512]{1,0:T(8,128)(2,1)}, bf16[1024,512]{1,0:T(8,128)(2,1)S(1)}, u32[]{:S(2)}, u32[]{:S(2)}) collective-permute-start(bf16[1024,512]{1,0:T(8,128)(2,1)} %all-gather.6.cloned.1.call-done), channel_id=1, source_target_pairs={{0,128},{128,256},{256,384},{384,0},{1,129},{129,257},{257,385},{3... | collective-permute-start | bytes 3145736 | tf_op jit(solution)/shard_map/ppermute | solution.py:15
  201.8 55.1 %collective-permute-done = bf16[1024,512]{1,0:T(8,128)(2,1)S(1)} collective-permute-done((bf16[1024,512]{1,0:T(8,128)(2,1)}, bf16[1024,512]{1,0:T(8,128)(2,1)S(1)}, u32[]{:S(2)}, u32[]{:S(2)}) %collective-permute-start) | collective-permute-done | bytes 1048608 | tf_op jit(solution)/shard_map/ppermute | solution.py:15
  256.9 1.7 convolution_convert_fusion
  258.6 0.0 all-gather.10.cloned.1.call-start
  258.7 1.3 convolution_convert_fusion.1
  260.0 0.1 iota_compare_fusion
  260.1 0.2 multiply_cosine_fusion.1
  260.3 0.3 fusion.4
  260.6 73.4 %psum.14 = bf16[1024]{0:T(1024)(128)(2,1)S(1)} all-reduce(bf16[1024]{0:T(1024)(128)(2,1)S(1)} %fusion.4), channel_id=1, replica_groups=mesh['section'=4,'dp'=8,'tensor'=16] {'tensor'}, use_global_device_ids=true, to_apply=%region_3.0 | all-reduce | flops 1024 | bytes 4096 | tf_op jit(solution)/shard_map/psum | solution.py:58
  334.0 0.1 dynamic-slice.3
  334.0 124.3 %all-reduce.2.cloned.1.call-done = bf16[1024,512]{1,0:T(8,128)(2,1)} async-done(((bf16[1024,512]{1,0:T(8,128)(2,1)}), bf16[1024,512]{1,0:T(8,128)(2,1)}) %all-reduce.2.cloned.1.call-update) | async-done | bytes 1048592 | tf_op jit(solution)/shard_map/psum | solution.py:54
  458.4 0.9 convert_multiply_fusion.2
  459.4 0.1 fusion.39
  459.5 117.3 %all-gather.10.cloned.1.call-done = bf16[16384,256]{1,0:T(8,128)(2,1)} async-done(((bf16[1024,256]{1,0:T(8,128)(2,1)}), bf16[16384,256]{1,0:T(8,128)(2,1)}) %all-gather.10.cloned.1.call-update) | async-done | bytes 8388624 | tf_op jit(solution)/shard_map/all_gather | solution.py:55
  576.8 4.8 reduce_sum.30
  581.6 0.2 copy.13
  581.8 0.3 copy.14
  582.2 0.2 broadcast_multiply_fusion
  582.4 2.4 fusion.33
  584.9 0.5 fusion.40
  585.3 0.3 fusion.13
  585.7 0.4 fusion.12
  586.0 0.1 copy.17
  586.1 0.7 broadcast_in_dim_reshape.3
  (21 shorter events, 0.3 us)
Async XLA Ops:
  6.5 250.4 %copy-start = (bf16[1,512,512]{2,1,0:T(8,128)(2,1)S(1)}, bf16[1,512,512]{2,1,0:T(8,128)(2,1)}, u32[]{:S(2)}) copy-start(bf16[1,512,512]{2,1,0:T(8,128)(2,1)} %param.10) | copy-start | bytes 1572868
  6.5 103.6 %all-gather.8.cloned.1.call-start = ((), (), s32[]{:S(2)}) async-start(), calls=%async_computation.4 | async-start | bytes 7798784 | tf_op jit(solution)/shard_map/all_gather | solution.py:35
  7.3 153.0 %copy-start.1 = (bf16[1,128,512]{2,1,0:T(8,128)(2,1)S(1)}, bf16[1,128,512]{2,1,0:T(8,128)(2,1)}, u32[]{:S(2)}) copy-start(bf16[1,128,512]{2,1,0:T(8,128)(2,1)} %param.8) | copy-start | bytes 393220
  7.3 249.6 %copy-start.3 = (f32[1,512]{1,0:T(1,128)S(1)}, f32[1,512]{1,0:T(1,128)}, u32[]{:S(2)}) copy-start(f32[1,512]{1,0:T(1,128)} %param.9) | copy-start | bytes 6148
  7.3 153.0 %reduce-scatter.2.cloned.1.call-start = ((), (), s32[]{:S(2)}) async-start(), calls=%async_computation.1 | async-start | bytes 1179648 | tf_op jit(solution)/shard_map/reduce_scatter | solution.py:39
  119.3 75.4 %all-gather.6.cloned.1.call-start = ((), (), s32[]{:S(2)}) async-start(), calls=%async_computation.2 | async-start | bytes 1179648 | tf_op jit(solution)/shard_map/all_gather | solution.py:43
  161.9 296.5 %all-reduce.2.cloned.1.call-start = ((), (), s32[]{:S(2)}) async-start(), calls=%async_computation.3 | async-start | bytes 2097152 | tf_op jit(solution)/shard_map/psum | solution.py:54
  194.6 62.3 %collective-permute-start = (bf16[1024,512]{1,0:T(8,128)(2,1)}, bf16[1024,512]{1,0:T(8,128)(2,1)S(1)}, u32[]{:S(2)}, u32[]{:S(2)}) collective-permute-start(bf16[1024,512]{1,0:T(8,128)(2,1)} %all-gather.6.cloned.1.call-done), channel_id=1, source_target_pairs={{0,128},{128,256},{256,384},{384,0},{1,129},{129,257},{257,385},{3... | collective-permute-start | bytes 3145736 | tf_op jit(solution)/shard_map/ppermute | solution.py:15
  256.9 1.8 copy-start.2
  258.6 318.2 %all-gather.10.cloned.1.call-start = ((), (), s32[]{:S(2)}) async-start(), calls=%async_computation.5 | async-start | bytes 8912896 | tf_op jit(solution)/shard_map/all_gather | solution.py:55
Sparse Core Ops, SparseCore 0:
  9.4 100.6 all-gather.7
  119.4 40.8 reduce-scatter.1
  162.4 32.1 all-gather.5
  258.7 199.5 all-reduce.1
  460.5 116.2 all-gather.9
